TPU v7x, 256 devices: a whole 4x4x8 slice. The times are simulated.
256 devices in a mesh: seq: 32 (over y, z), head: 8 (over x, core).
Axes of the slice: x: 4, y: 4, z: 8, core: 2. Of those that a mesh axis runs over, the one named last changes fastest.
Arguments:
- tokens: bfloat16 [16384, 2048], P('seq'), may hold values from -24 to 24
- w_query: bfloat16 [2048, 2048], P(None, 'head'), may hold values from -0.125 to 0.125
- w_key: bfloat16 [2048, 2048], P(None, 'head'), may hold values from -0.125 to 0.125
- w_value: bfloat16 [2048, 2048], P(None, 'head'), may hold values from -0.125 to 0.125
- w_out: bfloat16 [2048, 2048], P('head'), may hold values from -0.125 to 0.125
- shared_gate: bfloat16 [2048, 1024], P(None, 'head'), may hold values from -0.125 to 0.125
- shared_up: bfloat16 [2048, 1024], P(None, 'head'), may hold values from -0.125 to 0.125
- shared_down: bfloat16 [1024, 2048], P('head'), may hold values from -0.1875 to 0.1875
- expert_gate: bfloat16 [64, 2048, 1024], P('seq', None, 'head'), may hold values from -0.125 to 0.125
- expert_up: bfloat16 [64, 2048, 1024], P('seq', None, 'head'), may hold values from -0.125 to 0.125
- expert_down: bfloat16 [64, 1024, 2048], P('seq', 'head'), may hold values from -0.1875 to 0.1875
- expert_ids: int32 [16384, 1], P('seq'), may hold values from 0 to 63; in each aligned block of 512 rows (0 to 511, 512 to 1023, ...) at most 16 rows name the same one
Outputs:
- output: bfloat16 [16384, 2048], P('seq', 'head')
Inputs may be any that keep to these rules, and one draw needn't show every extreme that they name: `expert_ids`: among the 512 tokens of one index of seq (aligned blocks of the sequence) at most 16 name the same expert, and in some block of every draw one expert is named by exactly 16 tokens.
All inputs are finite; a program needn't handle non-finite values.
Results may differ from a plain program's by a relative error of at most 0.015.
Values may be sent and summed in bfloat16 or wider, within the bound.
A program may use at most 128 MiB of HBM per device.

v0:
```python
import jax
import jax.numpy as jnp
from jax import lax
from jax.sharding import PartitionSpec as P

HD = 128
EXPERTS = 64
CAP = 16
F32 = jnp.float32
BF16 = jnp.bfloat16


def dot(a, b):
    return jnp.dot(a, b, preferred_element_type=F32)


def two_part(values):
    high = values.astype(BF16)
    return (high, (values - high.astype(F32)).astype(BF16))


def head_columns(weights):
    return lax.all_to_all(weights, "head", split_axis=1, concat_axis=0, tiled=True)


def gather_columns(block):
    return lax.all_gather(block, "head", axis=1, tiled=True)


def carried_state(local_state):
    shape = local_state.shape
    length = lax.axis_size("seq")
    chunks = local_state.reshape(length, -1, HD)
    mine = lax.all_to_all(chunks, "seq", split_axis=0, concat_axis=0, tiled=True)
    earlier = jnp.arange(length)[:, None] > jnp.arange(length)[None, :]
    before = jnp.sum(jnp.where(earlier[:, :, None, None], mine[None], 0.0), axis=1)
    back = lax.all_to_all(before, "seq", split_axis=0, concat_axis=0, tiled=True)
    return back.reshape(shape)


def row_scale(rows):
    wide = rows.astype(F32)
    return lax.rsqrt(jnp.mean(wide * wide, axis=-1, keepdims=True) + 1e-06)


def shards(
    tokens,
    w_query,
    w_key,
    w_value,
    w_out,
    shared_gate,
    shared_up,
    shared_down,
    expert_gate,
    expert_up,
    expert_down,
    expert_ids,
):
    rows, width = tokens.shape
    heads = w_query.shape[1] // HD
    owned = expert_gate.shape[0]
    sources = lax.axis_size("seq")
    experts = owned * sources
    cols = width // lax.axis_size("head")
    head = lax.axis_index("head")
    out_cols = head_columns(w_out)
    shared_cols = head_columns(shared_down)
    expert_cols = lax.all_to_all(expert_down, "head", split_axis=2, concat_axis=1, tiled=True)
    inputs = tokens.astype(F32)
    normed = (inputs * row_scale(tokens)).astype(BF16)
    query = dot(normed, w_query).astype(BF16).reshape(rows, heads, HD)
    key = dot(normed, w_key).astype(BF16).reshape(rows, heads, HD)
    value = dot(normed, w_value).astype(BF16).reshape(rows, heads, HD)
    state = jnp.einsum("thd,the->hde", key, value, preferred_element_type=F32)
    carried = carried_state(state)
    causal = jnp.arange(rows)[:, None] >= jnp.arange(rows)[None, :]
    scores = jnp.einsum("thd,shd->hts", query, key, preferred_element_type=F32)
    scores = two_part(jnp.where(causal[None], scores, 0.0))
    carried = two_part(carried)
    attended = sum(
        (jnp.einsum("hts,shd->thd", part, value, preferred_element_type=F32) for part in scores)
    ) + sum(
        (jnp.einsum("thd,hde->the", query, part, preferred_element_type=F32) for part in carried)
    )
    head_normed = (
        (attended * lax.rsqrt(jnp.mean(attended * attended, axis=-1, keepdims=True) + 1e-06))
        .astype(BF16)
        .reshape(rows, heads * HD)
    )
    own_tokens = lax.dynamic_slice_in_dim(tokens, head * cols, cols, 1)
    residual = own_tokens.astype(F32) + dot(gather_columns(head_normed), out_cols)
    sent = residual.astype(BF16)
    expert_of = expert_ids[:, 0]
    same = (expert_of[:, None] == expert_of[None, :]) & causal
    rank = jnp.sum(same.astype(jnp.int32), axis=1) - 1
    slot = expert_of * CAP + rank
    chosen = jnp.arange(experts * CAP, dtype=jnp.int32)[:, None] == slot[None, :]
    chosen = chosen.astype(BF16)
    outgoing = dot(chosen, sent).astype(BF16).reshape(sources, owned, CAP, cols)
    arrived = lax.all_to_all(outgoing, "seq", split_axis=0, concat_axis=0, tiled=True)
    arrived = arrived.transpose(1, 0, 2, 3).reshape(owned * sources * CAP, cols)
    routed_in = gather_columns(arrived)
    middle = gather_columns(sent)
    scale = row_scale(middle)
    shared_hidden = (
        jax.nn.silu(dot(middle, shared_gate) * scale) * (dot(middle, shared_up) * scale)
    ).astype(BF16)
    scale = row_scale(routed_in).reshape(owned, sources * CAP, 1)
    routed_in = routed_in.reshape(owned, sources * CAP, width)
    gate = jnp.einsum("erd,edf->erf", routed_in, expert_gate, preferred_element_type=F32)
    up = jnp.einsum("erd,edf->erf", routed_in, expert_up, preferred_element_type=F32)
    routed_hidden = (jax.nn.silu(gate * scale) * (up * scale)).astype(BF16)
    both = jnp.concatenate([shared_hidden, routed_hidden.reshape(owned * sources * CAP, -1)])
    both = gather_columns(both)
    shared_out = dot(both[:rows], shared_cols)
    routed_out = jnp.einsum(
        "erf,efd->erd",
        both[rows:].reshape(owned, sources * CAP, -1),
        expert_cols,
        preferred_element_type=F32,
    ).astype(BF16)
    routed_out = routed_out.reshape(owned, sources, CAP, cols).transpose(1, 0, 2, 3)
    returned = lax.all_to_all(routed_out, "seq", split_axis=0, concat_axis=0, tiled=True)
    returned = returned.reshape(experts * CAP, cols)
    routed = lax.dot_general(chosen, returned, (((0,), (0,)), ((), ())), preferred_element_type=F32)
    return (residual + shared_out + routed).astype(BF16)


def solution(mesh):
    return jax.shard_map(
        shards,
        mesh=mesh,
        in_specs=(
            P("seq", None),
            P(None, "head"),
            P(None, "head"),
            P(None, "head"),
            P("head", None),
            P(None, "head"),
            P(None, "head"),
            P("head", None),
            P("seq", None, "head"),
            P("seq", None, "head"),
            P("seq", "head", None),
            P("seq", None),
        ),
        out_specs=P("seq", "head"),
        check_vma=False,
    )
```

profile of v0, /device:TPU:32, one launch (start us, length us, event | category | flops | bytes accessed | tf_op | source)
XLA Modules:
  0.0 251.0 jit_solution(1890059835473310391)
XLA Ops:
  6.5 2.2 fusion
  8.8 0.3 copy-done.5
  9.1 0.9 convolution_convert_fusion.1
  10.0 0.3 copy-done.17
  10.3 0.9 convolution_convert_fusion.3
  11.3 0.9 fusion.31
  12.1 11.4 %all-to-all-start = ((f32[32,8,128]{2,1,0:T(8,128)}), f32[32,8,128]{2,1,0:T(8,128)S(1)}, u32[]{:S(2)}, u32[]{:S(2)}) async-start(f32[32,8,128]{2,1,0:T(8,128)} %bitcast.3), calls=%async_computation | async-start | bytes 262144 | tf_op jit(solution)/shard_map/all_to_all | solution.py:34
  23.5 0.8 iota_compare_fusion.5
  24.3 2.1 convolution_convert_fusion.2
  26.5 0.7 copy-done.4
  27.2 0.5 fusion.30
  27.6 5.7 %all-to-all-done = f32[32,8,128]{2,1,0:T(8,128)S(1)} async-done(((f32[32,8,128]{2,1,0:T(8,128)}), f32[32,8,128]{2,1,0:T(8,128)S(1)}, u32[]{:S(2)}, u32[]{:S(2)}) %all-to-all-start) | async-done | bytes 131104 | tf_op jit(solution)/shard_map/all_to_all | solution.py:34
  33.3 2.1 select_reduce_fusion
  35.4 4.3 %all-to-all-start.1 = ((f32[32,8,128]{2,1,0:T(8,128)}), f32[32,8,128]{2,1,0:T(8,128)S(1)}, u32[]{:S(2)}, u32[]{:S(2)}) async-start(f32[32,8,128]{2,1,0:T(8,128)} %select_reduce_fusion), calls=%async_computation.1 | async-start | bytes 262144 | tf_op jit(solution)/shard_map/all_to_all | solution.py:37
  39.6 0.0 all-gather.5.cloned.1.call-start
  39.7 2.3 fusion.4
  42.0 7.5 %all-to-all-done.1 = f32[32,8,128]{2,1,0:T(8,128)S(1)} async-done(((f32[32,8,128]{2,1,0:T(8,128)}), f32[32,8,128]{2,1,0:T(8,128)S(1)}, u32[]{:S(2)}, u32[]{:S(2)}) %all-to-all-start.1) | async-done | bytes 131104 | tf_op jit(solution)/shard_map/all_to_all | solution.py:37
  49.5 0.7 copy-done.14
  50.1 1.0 copy.61
  51.1 1.2 fusion.22
  52.4 1.2 convolution_add_fusion.3
  53.5 0.6 multiply_reduce_fusion.2
  54.2 0.7 multiply_convert_fusion
  54.9 0.0 all-gather.5.cloned.1.call-update
  54.9 2.3 copy.65
  57.2 4.3 %all-to-all-start.2 = ((bf16[256,8,256]{0,2,1:T(8,128)(2,1)}), bf16[256,8,256]{0,2,1:T(8,128)(2,1)S(1)}, u32[]{:S(2)}, u32[]{:S(2)}) async-start(bf16[256,8,256]{0,2,1:T(8,128)(2,1)} %bitcast.7), calls=%async_computation.2 | async-start | bytes 2097152 | tf_op jit(solution)/shard_map/all_to_all | solution.py:23
  61.5 0.0 all-gather.7.cloned.1.call-start
  61.6 24.3 %all-to-all-done.2 = bf16[256,8,256]{0,2,1:T(8,128)(2,1)S(1)} async-done(((bf16[256,8,256]{0,2,1:T(8,128)(2,1)}), bf16[256,8,256]{0,2,1:T(8,128)(2,1)S(1)}, u32[]{:S(2)}, u32[]{:S(2)}) %all-to-all-start.2) | async-done | bytes 1048608 | tf_op jit(solution)/shard_map/all_to_all | solution.py:23
  85.9 0.5 copy.66
  86.4 0.0 all-gather.5.cloned.1.call-done
  86.4 3.2 %fusion.29 = (bf16[512,256]{1,0:T(8,128)(2,1)}, f32[512,256]{1,0:T(8,128)}) fusion(bf16[512,2048]{0,1:T(8,128)(2,1)} %all-gather.5.cloned.1.call-done, bf16[2048,256]{1,0:T(8,128)(2,1)S(1)} %bitcast.73, bf16[512,2048]{1,0:T(8,128)(2,1)} %param.12, s32[]{:T(128)S(6)} %select_n.11), kind=kOutput, calls=%fused_computation.59 | convolution fusion | flops 537264128 | bytes 4194308 | tf_op jit(solution)/shard_map/dot_general | solution.py:14
  89.7 0.0 all-gather.7.cloned.1.call-update
  89.7 0.0 all-gather.9.cloned.1.call-start
  89.7 0.2 convert_reduce_fusion
  90.0 1.4 fusion.5
  91.4 23.0 %all_to_all.76 = bf16[32,2,16,256]{3,2,1,0:T(8,128)(2,1)S(1)} all-to-all(bf16[32,2,16,256]{3,2,1,0:T(8,128)(2,1)S(1)} %bitcast.77), channel_id=1, replica_groups=mesh['seq'=32,'head'=8] {'seq'}, dimensions={0} | all-to-all | bytes 1048576 | tf_op jit(solution)/shard_map/all_to_all | solution.py:101
  114.5 0.8 copy.67
  115.3 0.2 all-gather.11.cloned.1.call-start
  115.5 0.0 all-gather.7.cloned.1.call-done
  115.6 2.2 multiply_reduce_fusion.1
  117.8 0.7 convolution_multiply_fusion.3
  118.6 0.7 fusion.13
  119.3 36.5 %all-gather.9.cloned.1.call-done = bf16[1024,2048]{1,0:T(8,128)(2,1)} async-done(((bf16[1024,256]{1,0:T(8,128)(2,1)}), bf16[1024,2048]{1,0:T(8,128)(2,1)}) %all-gather.9.cloned.1.call-update) | async-done | bytes 4194320 | tf_op jit(solution)/shard_map/all_gather | solution.py:27
  155.7 3.1 %multiply_reduce_fusion = f32[1024]{0:T(1024)S(1)} fusion(bf16[1024,2048]{1,0:T(8,128)(2,1)} %all-gather.9.cloned.1.call-done), kind=kLoop, calls=%fused_computation | loop fusion | flops 6290432 | bytes 4198400 | tf_op jit(solution)/shard_map/reduce_sum | solution.py:43
  158.9 3.6 %convolution_multiply_fusion.1 = f32[2,512,128]{2,1,0:T(8,128)S(1)} fusion(bf16[2,512,2048]{2,1,0:T(8,128)(2,1)} %bitcast.57, bf16[2,2048,128]{2,1,0:T(8,128)(2,1)S(1)} %copy-done.11, f32[2,512]{1,0:T(2,128)S(1)} %rsqrt.40), kind=kOutput, calls=%fused_computation.23 | convolution fusion | flops 537001984 | bytes 5771264 | tf_op jit(solution)/shard_map/erd,edf->erf/dot_general | solution.py:111
  162.5 0.1 copy-done.18
  162.6 1.3 fusion.10
  163.9 0.8 pad_maximum_fusion
  164.7 2.0 copy.70
  166.7 3.9 %all-to-all-start.5 = ((bf16[2,128,2048]{1,0,2:T(2,128)(2,1)}), bf16[2,128,2048]{1,0,2:T(2,128)(2,1)S(1)}, u32[]{:S(2)}, u32[]{:S(2)}) async-start(bf16[2,128,2048]{1,0,2:T(2,128)(2,1)} %copy.70), calls=%async_computation.5 | async-start | bytes 2097152 | tf_op jit(solution)/shard_map/all_to_all | solution.py:69
  170.7 1.0 copy.68
  171.7 19.1 %all-to-all-done.5 = bf16[2,128,2048]{1,0,2:T(2,128)(2,1)S(1)} async-done(((bf16[2,128,2048]{1,0,2:T(2,128)(2,1)}), bf16[2,128,2048]{1,0,2:T(2,128)(2,1)S(1)}, u32[]{:S(2)}, u32[]{:S(2)}) %all-to-all-start.5) | async-done | bytes 1048608 | tf_op jit(solution)/shard_map/all_to_all | solution.py:69
  190.8 4.1 %all-to-all-start.4 = ((bf16[128,8,256]{0,2,1:T(8,128)(2,1)}), bf16[128,8,256]{0,2,1:T(8,128)(2,1)}, u32[]{:S(2)}, u32[]{:S(2)}) async-start(bf16[128,8,256]{0,2,1:T(8,128)(2,1)} %bitcast.16), calls=%async_computation.4 | async-start | bytes 1048576 | tf_op jit(solution)/shard_map/all_to_all | solution.py:23
  195.0 2.0 copy.71
  197.0 12.7 %all-gather.11.cloned.1.call-done = bf16[1536,1024]{1,0:T(8,128)(2,1)} async-done(((bf16[1536,128]{1,0:T(8,128)(2,1)}), bf16[1536,1024]{1,0:T(8,128)(2,1)}) %all-gather.11.cloned.1.call-update) | async-done | bytes 3145744 | tf_op jit(solution)/shard_map/all_gather | solution.py:27
  209.7 1.6 slice-done
  211.2 0.3 copy-done.10
  211.5 0.7 convolution_convert_fusion
  212.2 0.9 copy.79
  213.1 10.2 %all-to-all-start.6 = ((bf16[32,2,16,256]{3,2,1,0:T(8,128)(2,1)}), bf16[32,2,16,256]{3,2,1,0:T(8,128)(2,1)S(1)}, u32[]{:S(2)}, u32[]{:S(2)}) async-start(bf16[32,2,16,256]{3,2,1,0:T(8,128)(2,1)} %bitcast.56), calls=%async_computation.6 | async-start | bytes 1048576 | tf_op jit(solution)/shard_map/all_to_all | solution.py:124
  223.3 1.2 copy.69
  224.6 16.8 %all-to-all-done.6 = bf16[32,2,16,256]{3,2,1,0:T(8,128)(2,1)S(1)} async-done(((bf16[32,2,16,256]{3,2,1,0:T(8,128)(2,1)}), bf16[32,2,16,256]{3,2,1,0:T(8,128)(2,1)S(1)}, u32[]{:S(2)}, u32[]{:S(2)}) %all-to-all-start.6) | async-done | bytes 524320 | tf_op jit(solution)/shard_map/all_to_all | solution.py:124
  241.4 0.7 fusion.2
  242.1 2.4 fusion.11
  (45 shorter events, 0.2 us)
Async XLA Ops:
  6.5 2.2 copy-start
  6.5 2.5 %copy-start.5 = (bf16[512,2048]{1,0:T(8,128)(2,1)S(1)}, bf16[512,2048]{1,0:T(8,128)(2,1)}, u32[]{:S(2)}) copy-start(bf16[512,2048]{1,0:T(8,128)(2,1)} %param.12) | copy-start | bytes 6291460
  9.1 1.2 copy-start.17
  10.3 0.9 copy-start.7
  12.1 21.2 %all-to-all-start = ((f32[32,8,128]{2,1,0:T(8,128)}), f32[32,8,128]{2,1,0:T(8,128)S(1)}, u32[]{:S(2)}, u32[]{:S(2)}) async-start(f32[32,8,128]{2,1,0:T(8,128)} %bitcast.3), calls=%async_computation | async-start | bytes 262144 | tf_op jit(solution)/shard_map/all_to_all | solution.py:34
  24.3 2.8 %copy-start.8 = (bf16[512,256]{0,1:T(8,128)(2,1)S(1)}, bf16[512,256]{0,1:T(8,128)(2,1)}, u32[]{:S(2)}) copy-start(bf16[512,256]{0,1:T(8,128)(2,1)} %copy-done.7) | copy-start | bytes 786436
  26.4 0.7 copy-start.4
  35.4 14.1 %all-to-all-start.1 = ((f32[32,8,128]{2,1,0:T(8,128)}), f32[32,8,128]{2,1,0:T(8,128)S(1)}, u32[]{:S(2)}, u32[]{:S(2)}) async-start(f32[32,8,128]{2,1,0:T(8,128)} %select_reduce_fusion), calls=%async_computation.1 | async-start | bytes 262144 | tf_op jit(solution)/shard_map/all_to_all | solution.py:37
  39.6 46.8 %all-gather.5.cloned.1.call-start = ((), (), s32[]{:S(2)}) async-start(), calls=%async_computation.7 | async-start | bytes 2359296 | tf_op jit(solution)/shard_map/all_gather | solution.py:27
  49.4 0.7 copy-start.14
  51.1 2.4 copy-start.3
  51.1 2.4 copy-start.6
  57.2 28.7 %all-to-all-start.2 = ((bf16[256,8,256]{0,2,1:T(8,128)(2,1)}), bf16[256,8,256]{0,2,1:T(8,128)(2,1)S(1)}, u32[]{:S(2)}, u32[]{:S(2)}) async-start(bf16[256,8,256]{0,2,1:T(8,128)(2,1)} %bitcast.7), calls=%async_computation.2 | async-start | bytes 2097152 | tf_op jit(solution)/shard_map/all_to_all | solution.py:23
  61.5 54.1 %all-gather.7.cloned.1.call-start = ((), (), s32[]{:S(2)}) async-start(), calls=%async_computation.8 | async-start | bytes 2359296 | tf_op jit(solution)/shard_map/all_gather | solution.py:27
  86.4 3.3 %copy-start.16 = (s32[512,1]{0,1:T(1,128)S(1)}, s32[512,1]{0,1:T(1,128)}, u32[]{:S(2)}) copy-start(s32[512,1]{0,1:T(1,128)} %param.23) | copy-start | bytes 6148
  89.7 66.1 %all-gather.9.cloned.1.call-start = ((), (), s32[]{:S(2)}) async-start(), calls=%async_computation.9 | async-start | bytes 4718592 | tf_op jit(solution)/shard_map/all_gather | solution.py:27
  114.5 3.4 %copy-start.12 = (bf16[2048,128]{1,0:T(8,128)(2,1)S(1)}, bf16[2048,128]{1,0:T(8,128)(2,1)}, u32[]{:S(2)}) copy-start(bf16[2048,128]{1,0:T(8,128)(2,1)} %param.17) | copy-start | bytes 1572868
  115.3 3.3 %copy-start.19 = (bf16[2048,128]{1,0:T(8,128)(2,1)S(1)}, bf16[2048,128]{1,0:T(8,128)(2,1)}, u32[]{:S(2)}) copy-start(bf16[2048,128]{1,0:T(8,128)(2,1)} %param.18) | copy-start | bytes 1572868
  115.3 94.3 %all-gather.11.cloned.1.call-start = ((), (), s32[]{:S(2)}) async-start(), calls=%async_computation.10 | async-start | bytes 3538944 | tf_op jit(solution)/shard_map/all_gather | solution.py:27
  115.6 2.3 copy-start.2
  119.3 39.6 %copy-start.11 = (bf16[2,2048,128]{2,1,0:T(8,128)(2,1)S(1)}, bf16[2,2048,128]{2,1,0:T(8,128)(2,1)}, u32[]{:S(2)}) copy-start(bf16[2,2048,128]{2,1,0:T(8,128)(2,1)} %param.20) | copy-start | bytes 3145732
  158.9 3.6 %copy-start.1 = (bf16[1024,2048]{1,0:T(8,128)(2,1)S(1)}, bf16[1024,2048]{1,0:T(8,128)(2,1)}, u32[]{:S(2)}) copy-start(bf16[1024,2048]{1,0:T(8,128)(2,1)} %all-gather.9.cloned.1.call-done) | copy-start | bytes 12582916
  158.9 3.7 %copy-start.18 = (bf16[2,2048,128]{2,1,0:T(8,128)(2,1)S(1)}, bf16[2,2048,128]{2,1,0:T(8,128)(2,1)}, u32[]{:S(2)}) copy-start(bf16[2,2048,128]{2,1,0:T(8,128)(2,1)} %param.21) | copy-start | bytes 3145732
  162.6 2.1 copy-start.9
  164.7 6.0 %copy-start.13 = (bf16[128,2048]{1,0:T(8,128)(2,1)S(1)}, bf16[128,2048]{1,0:T(8,128)(2,1)}, u32[]{:S(2)}) copy-start(bf16[128,2048]{1,0:T(8,128)(2,1)} %param.19) | copy-start | bytes 1572868
  166.7 24.1 %all-to-all-start.5 = ((bf16[2,128,2048]{1,0,2:T(2,128)(2,1)}), bf16[2,128,2048]{1,0,2:T(2,128)(2,1)S(1)}, u32[]{:S(2)}, u32[]{:S(2)}) async-start(bf16[2,128,2048]{1,0,2:T(2,128)(2,1)} %copy.70), calls=%async_computation.5 | async-start | bytes 2097152 | tf_op jit(solution)/shard_map/all_to_all | solution.py:69
  190.8 22.3 %all-to-all-start.4 = ((bf16[128,8,256]{0,2,1:T(8,128)(2,1)}), bf16[128,8,256]{0,2,1:T(8,128)(2,1)}, u32[]{:S(2)}, u32[]{:S(2)}) async-start(bf16[128,8,256]{0,2,1:T(8,128)(2,1)} %bitcast.16), calls=%async_computation.4 | async-start | bytes 1048576 | tf_op jit(solution)/shard_map/all_to_all | solution.py:23
  209.7 1.6 slice-start
  209.7 1.9 copy-start.10
  213.1 29.0 %copy-start.15 = (f32[512,256]{1,0:T(8,128)S(1)}, f32[512,256]{1,0:T(8,128)}, u32[]{:S(2)}) copy-start(f32[512,256]{1,0:T(8,128)} %get-tuple-element.8) | copy-start | bytes 1572868
  213.1 28.3 %all-to-all-start.6 = ((bf16[32,2,16,256]{3,2,1,0:T(8,128)(2,1)}), bf16[32,2,16,256]{3,2,1,0:T(8,128)(2,1)S(1)}, u32[]{:S(2)}, u32[]{:S(2)}) async-start(bf16[32,2,16,256]{3,2,1,0:T(8,128)(2,1)} %bitcast.56), calls=%async_computation.6 | async-start | bytes 1048576 | tf_op jit(solution)/shard_map/all_to_all | solution.py:124
Sparse Core Ops, SparseCore 0:
  55.1 29.5 all-gather.4
  89.8 25.0 all-gather.6
  116.7 39.0 all-gather.8
  164.8 44.8 all-gather.10
where the time goes:
time: 252 us; the launch traced here: 251 us
  waiting for transfers between devices  123 us (49%)
  starting transfers between devices  38.6 us (15%)
  matrix products  25.3 us (10%)
  blocking collectives  23 us (9%)
  local copies, waits for them, and re-layouts  15.8 us (6%)
  between operations  13.5 us (5%)
  other arithmetic  12.2 us (5%)
    all_gather x4, waiting for transfers between devices, gather_columns(): return lax.all_gather(block, 'head', axis=1, tiled=True)  49.2 us
    all_to_all x2, waiting for transfers between devices, head_columns(): lax.all_to_all(weights, 'head', split_axis=1, concat_axis=0, tiled=True)  24.3 us
    all_to_all x1, blocking collectives, shards(): lax.all_to_all(outgoing, 'seq', split_axis=0, concat_axis=0, tiled=True)  23 us
    all_to_all x1, waiting for transfers between devices, shards(): lax.all_to_all(expert_down, 'head', split_axis=2, concat_axis=1, tiled=True)  19.1 us
    all_to_all x1, waiting for transfers between devices, shards(): lax.all_to_all(routed_out, 'seq', split_axis=0, concat_axis=0, tiled=True)  16.8 us
    dot_general x8, matrix products, dot(): return jnp.dot(a, b, preferred_element_type=F32)  12.4 us
    all_to_all x1, starting transfers between devices, carried_state(): lax.all_to_all(chunks, 'seq', split_axis=0, concat_axis=0, tiled=True)  11.4 us
    all_to_all x1, starting transfers between devices, shards(): lax.all_to_all(routed_out, 'seq', split_axis=0, concat_axis=0, tiled=True)  10.2 us
  transfers between devices with their start and end apart: 10, of which 7 were waited for; matrix products, arithmetic and copies ran while one was open for 9% of the time, Pallas kernels for 0%

commit v1 on v0

--- a/solution.py
+++ b/solution.py
@@ -24,7 +24,9 @@
 
 
 def gather_columns(block):
-    return lax.all_gather(block, "head", axis=1, tiled=True)
+    return jnp.concatenate(
+        lax.all_to_all(jnp.stack([block] * lax.axis_size("head")), "head", 0, 0), axis=1
+    )
 
 
 def carried_state(local_state):

time: 252 us -> 325 us (1.29)
  waiting for transfers between devices: 123 us -> 195 us
  blocking collectives: 23 us -> 0 us
  local copies, waits for them, and re-layouts: 15.8 us -> 38.1 us
  starting transfers between devices: 38.6 us -> 56.5 us
  between operations: 13.5 us -> 0.41 us
    all_to_all x0 -> x5, waiting for transfers between devices: none -> 154 us  [the longest x4 136 us: gather_columns(): lax.all_to_all(jnp.stack([block] * lax.axis_size('head')), 'head', 0, 0)]
    all_gather x4 -> x0, waiting for transfers between devices: 49.2 us -> none  [gather_columns(): return lax.all_gather(block, 'head', axis=1, tiled=True)]
    all_to_all x1 -> x0, blocking collectives: 23 us -> none  [shards(): lax.all_to_all(outgoing, 'seq', split_axis=0, concat_axis=0, tiled=True)]
    all_to_all x0 -> x5, starting transfers between devices: none -> 21.3 us  [the longest x4 16.9 us: gather_columns(): lax.all_to_all(jnp.stack([block] * lax.axis_size('head')), 'head', 0, 0)]
    all_to_all x1, waiting for transfers between devices: 19.1 us -> 0.01 us  [shards(): lax.all_to_all(expert_down, 'head', split_axis=2, concat_axis=1, tiled=True)]
    another operation x0 -> x6, local copies, waits for them, and re-layouts: none -> 14.9 us  [the longest x5 7.47 us: gather_columns(): jnp.stack([block] * lax.axis_size('head'))]
    all_to_all x2, waiting for transfers between devices: 24.3 us -> 14.1 us  [head_columns(): lax.all_to_all(weights, 'head', split_axis=1, concat_axis=0, tiled=True)]
    reshape x0 -> x2, local copies, waits for them, and re-layouts: none -> 8.86 us  [the longest x1 6.57 us: gather_columns(): jnp.concatenate(lax.all_to_all(jnp.stack([block] * lax.axis_size('head'))...]
  transfers between devices with their start and end apart: 10 -> 11, of which waited for: 7 -> 9; matrix products, arithmetic and copies ran while one was open for 9% -> 15% of each run, Pallas kernels for 0% -> 0%
where the time goes in v1:
time: 325 us; the launch traced here: 324 us
  waiting for transfers between devices  195 us (60%)
  starting transfers between devices  56.5 us (17%)
  local copies, waits for them, and re-layouts  38.1 us (12%)
  matrix products  24.3 us (7%)
  other arithmetic  9.01 us (3%)
    all_to_all x4, waiting for transfers between devices, gather_columns(): lax.all_to_all(jnp.stack([block] * lax.axis_size('head')), 'head', 0, 0)  136 us
    all_to_all x1, waiting for transfers between devices, shards(): lax.all_to_all(outgoing, 'seq', split_axis=0, concat_axis=0, tiled=True)  17.6 us
    all_to_all x4, starting transfers between devices, gather_columns(): lax.all_to_all(jnp.stack([block] * lax.axis_size('head')), 'head', 0, 0)  16.9 us
    all_to_all x1, waiting for transfers between devices, shards(): lax.all_to_all(routed_out, 'seq', split_axis=0, concat_axis=0, tiled=True)  16.2 us
    all_to_all x2, waiting for transfers between devices, head_columns(): lax.all_to_all(weights, 'head', split_axis=1, concat_axis=0, tiled=True)  14.1 us
    all_to_all x1, starting transfers between devices, carried_state(): lax.all_to_all(chunks, 'seq', split_axis=0, concat_axis=0, tiled=True)  11.4 us
    dot_general x8, matrix products, dot(): return jnp.dot(a, b, preferred_element_type=F32)  10.8 us
    all_to_all x2, starting transfers between devices, head_columns(): lax.all_to_all(weights, 'head', split_axis=1, concat_axis=0, tiled=True)  8.45 us
  transfers between devices with their start and end apart: 11, of which 9 were waited for; matrix products, arithmetic and copies ran while one was open for 15% of the time, Pallas kernels for 0%

profile of v1, /device:TPU:32, one launch (start us, length us, event | category | flops | bytes accessed | tf_op | source)
XLA Modules:
  0.0 323.7 jit_solution(11328402177264562705)
XLA Ops:
  0.0 2.2 fusion
  2.2 0.3 copy-done.5
  2.6 0.9 convolution_convert_fusion.1
  3.4 0.3 copy-done.15
  3.8 0.9 convolution_convert_fusion.3
  4.7 0.9 fusion.42
  5.6 11.4 %all-to-all-start = ((f32[32,8,128]{2,1,0:T(8,128)}), f32[32,8,128]{2,1,0:T(8,128)S(1)}, u32[]{:S(2)}, u32[]{:S(2)}) async-start(f32[32,8,128]{2,1,0:T(8,128)} %bitcast.3), calls=%async_computation | async-start | bytes 262144 | tf_op jit(solution)/shard_map/all_to_all | solution.py:36
  17.0 0.8 iota_compare_fusion.9
  17.8 1.6 convolution_convert_fusion.2
  19.3 1.5 copy.64
  20.8 1.3 copy.65
  22.1 1.5 fusion.41
  23.7 3.1 all-to-all-done
  26.8 2.0 select_reduce_fusion
  28.8 6.7 %all-to-all-start.1 = ((f32[32,8,128]{2,1,0:T(8,128)}), f32[32,8,128]{2,1,0:T(8,128)S(1)}, u32[]{:S(2)}, u32[]{:S(2)}) async-start(f32[32,8,128]{2,1,0:T(8,128)} %select_reduce_fusion), calls=%async_computation.1 | async-start | bytes 262144 | tf_op jit(solution)/shard_map/all_to_all | solution.py:39
  35.6 1.3 fusion.6
  36.9 8.4 %all-to-all-done.1 = f32[32,8,128]{2,1,0:T(8,128)S(1)} async-done(((f32[32,8,128]{2,1,0:T(8,128)}), f32[32,8,128]{2,1,0:T(8,128)S(1)}, u32[]{:S(2)}, u32[]{:S(2)}) %all-to-all-start.1) | async-done | bytes 131104 | tf_op jit(solution)/shard_map/all_to_all | solution.py:39
  45.3 4.3 %all-to-all-start.3 = ((bf16[256,8,256]{2,0,1:T(8,128)(2,1)}), bf16[256,8,256]{2,0,1:T(8,128)(2,1)}, u32[]{:S(2)}, u32[]{:S(2)}) async-start(bf16[256,8,256]{2,0,1:T(8,128)(2,1)} %copy.65), calls=%async_computation.3 | async-start | bytes 2097152 | tf_op jit(solution)/shard_map/all_to_all | solution.py:23
  49.7 0.2 fusion.33
  49.9 0.2 convolution_add_fusion.1
  50.1 0.6 copy-done.6
  50.7 0.6 multiply_reduce_fusion.2
  51.6 14.1 %all-to-all-done.3 = bf16[256,8,256]{2,0,1:T(8,128)(2,1)} async-done(((bf16[256,8,256]{2,0,1:T(8,128)(2,1)}), bf16[256,8,256]{2,0,1:T(8,128)(2,1)}, u32[]{:S(2)}, u32[]{:S(2)}) %all-to-all-start.3) | async-done | bytes 1048608 | tf_op jit(solution)/shard_map/all_to_all | solution.py:23
  65.6 1.5 stack.8
  67.1 3.7 %all-to-all-start.2 = ((bf16[8,512,256]{2,1,0:T(8,128)(2,1)}), bf16[8,512,256]{2,1,0:T(8,128)(2,1)S(1)}, u32[]{:S(2)}, u32[]{:S(2)}) async-start(bf16[8,512,256]{2,1,0:T(8,128)(2,1)} %stack.8), calls=%async_computation.2 | async-start | bytes 4194304 | tf_op jit(solution)/shard_map/all_to_all | solution.py:28
  70.9 0.2 convert_reduce_fusion
  71.1 26.8 %all-to-all-done.2 = bf16[8,512,256]{2,1,0:T(8,128)(2,1)S(1)} async-done(((bf16[8,512,256]{2,1,0:T(8,128)(2,1)}), bf16[8,512,256]{2,1,0:T(8,128)(2,1)S(1)}, u32[]{:S(2)}, u32[]{:S(2)}) %all-to-all-start.2) | async-done | bytes 2097184 | tf_op jit(solution)/shard_map/all_to_all | solution.py:28
  97.9 2.8 fusion.40
  100.7 1.3 fusion.7
  102.0 4.5 %all-to-all-start.5 = ((bf16[32,2,16,256]{3,2,1,0:T(8,128)(2,1)}), bf16[32,2,16,256]{3,2,1,0:T(8,128)(2,1)S(1)}, u32[]{:S(2)}, u32[]{:S(2)}) async-start(bf16[32,2,16,256]{3,2,1,0:T(8,128)(2,1)} %bitcast.15), calls=%async_computation.5 | async-start | bytes 1048576 | tf_op jit(solution)/shard_map/all_to_all | solution.py:103
  106.6 17.6 %all-to-all-done.5 = bf16[32,2,16,256]{3,2,1,0:T(8,128)(2,1)S(1)} async-done(((bf16[32,2,16,256]{3,2,1,0:T(8,128)(2,1)}), bf16[32,2,16,256]{3,2,1,0:T(8,128)(2,1)S(1)}, u32[]{:S(2)}, u32[]{:S(2)}) %all-to-all-start.5) | async-done | bytes 524320 | tf_op jit(solution)/shard_map/all_to_all | solution.py:103
  124.2 1.5 stack.9
  125.7 3.6 %all-to-all-start.4 = ((bf16[8,512,256]{1,2,0:T(8,128)(2,1)}), bf16[8,512,256]{1,2,0:T(8,128)(2,1)S(1)}, u32[]{:S(2)}, u32[]{:S(2)}) async-start(bf16[8,512,256]{1,2,0:T(8,128)(2,1)} %stack.9), calls=%async_computation.4 | async-start | bytes 4194304 | tf_op jit(solution)/shard_map/all_to_all | solution.py:28
  129.3 27.0 %all-to-all-done.4 = bf16[8,512,256]{1,2,0:T(8,128)(2,1)S(1)} async-done(((bf16[8,512,256]{1,2,0:T(8,128)(2,1)}), bf16[8,512,256]{1,2,0:T(8,128)(2,1)S(1)}, u32[]{:S(2)}, u32[]{:S(2)}) %all-to-all-start.4) | async-done | bytes 2097184 | tf_op jit(solution)/shard_map/all_to_all | solution.py:28
  156.4 2.3 stack.10
  158.7 4.7 %all-to-all-start.6 = ((bf16[8,1024,256]{2,1,0:T(8,128)(2,1)}), bf16[8,1024,256]{2,1,0:T(8,128)(2,1)}, u32[]{:S(2)}, u32[]{:S(2)}) async-start(bf16[8,1024,256]{2,1,0:T(8,128)(2,1)} %stack.10), calls=%async_computation.6 | async-start | bytes 8388608 | tf_op jit(solution)/shard_map/all_to_all | solution.py:28
  163.4 2.0 copy.72
  165.4 0.5 multiply_reduce_fusion.1
  165.9 0.5 copy-done.13
  166.4 0.7 convolution_multiply_fusion.3
  167.2 0.8 fusion.22
  168.0 45.0 %all-to-all-done.6 = bf16[8,1024,256]{2,1,0:T(8,128)(2,1)} async-done(((bf16[8,1024,256]{2,1,0:T(8,128)(2,1)}), bf16[8,1024,256]{2,1,0:T(8,128)(2,1)}, u32[]{:S(2)}, u32[]{:S(2)}) %all-to-all-start.6) | async-done | bytes 4194336 | tf_op jit(solution)/shard_map/all_to_all | solution.py:28
  213.0 3.7 %all-to-all-start.9 = ((bf16[2,128,2048]{1,0,2:T(2,128)(2,1)}), bf16[2,128,2048]{1,0,2:T(2,128)(2,1)S(1)}, u32[]{:S(2)}, u32[]{:S(2)}) async-start(bf16[2,128,2048]{1,0,2:T(2,128)(2,1)} %copy.72), calls=%async_computation.9 | async-start | bytes 2097152 | tf_op jit(solution)/shard_map/all_to_all | solution.py:71
  216.8 3.1 multiply_reduce_fusion
  219.9 6.6 %copy.68 = bf16[1024,8,256]{2,1,0:T(8,128)(2,1)} copy(bf16[1024,8,256]{2,0,1:T(8,128)(2,1)} %bitcast.18) | data formatting | bytes 8388608 | tf_op jit(solution)/shard_map/reshape | solution.py:27
  226.4 7.5 %reshape_reshape.3 = bf16[2,512,2048]{2,1,0:T(8,128)(2,1)} reshape(bf16[1024,8,256]{2,1,0:T(8,128)(2,1)} %copy.68) | data formatting | bytes 8388608 | tf_op jit(solution)/shard_map/reshape;reshape | solution.py:112
  233.9 3.6 %convolution_multiply_fusion.1 = f32[2,512,128]{2,1,0:T(8,128)S(1)} fusion(bf16[2,512,2048]{2,1,0:T(8,128)(2,1)} %reshape_reshape.3, bf16[2,2048,128]{2,1,0:T(8,128)(2,1)S(1)} %copy-done.10, f32[2,512]{1,0:T(2,128)S(1)} %rsqrt.40), kind=kOutput, calls=%fused_computation.25 | convolution fusion | flops 537001984 | bytes 5771264 | tf_op jit(solution)/shard_map/erd,edf->erf/dot_general | solution.py:113
  237.6 1.3 fusion.19
  239.0 2.1 stack.11
  241.0 4.9 %all-to-all-start.7 = ((bf16[8,1536,128]{2,1,0:T(8,128)(2,1)}), bf16[8,1536,128]{2,1,0:T(8,128)(2,1)}, u32[]{:S(2)}, u32[]{:S(2)}) async-start(bf16[8,1536,128]{2,1,0:T(8,128)(2,1)} %stack.11), calls=%async_computation.7 | async-start | bytes 6291456 | tf_op jit(solution)/shard_map/all_to_all | solution.py:28
  245.9 0.3 copy.69
  246.2 1.0 copy.70
  247.2 37.2 %all-to-all-done.7 = bf16[8,1536,128]{2,1,0:T(8,128)(2,1)} async-done(((bf16[8,1536,128]{2,1,0:T(8,128)(2,1)}), bf16[8,1536,128]{2,1,0:T(8,128)(2,1)}, u32[]{:S(2)}, u32[]{:S(2)}) %all-to-all-start.7) | async-done | bytes 3145760 | tf_op jit(solution)/shard_map/all_to_all | solution.py:28
  284.4 4.1 %all-to-all-start.8 = ((bf16[128,8,256]{2,0,1:T(8,128)(2,1)}), bf16[128,8,256]{2,0,1:T(8,128)(2,1)}, u32[]{:S(2)}, u32[]{:S(2)}) async-start(bf16[128,8,256]{2,0,1:T(8,128)(2,1)} %copy.70), calls=%async_computation.8 | async-start | bytes 1048576 | tf_op jit(solution)/shard_map/all_to_all | solution.py:23
  288.5 2.0 copy.73
  290.6 1.7 slice.11
  292.3 1.4 copy.71
  293.7 2.3 reshape.153
  296.0 2.4 convolution_convert_fusion
  298.3 0.8 copy.81
  299.2 4.9 %all-to-all-start.10 = ((bf16[32,2,16,256]{3,2,1,0:T(8,128)(2,1)}), bf16[32,2,16,256]{3,2,1,0:T(8,128)(2,1)S(1)}, u32[]{:S(2)}, u32[]{:S(2)}) async-start(bf16[32,2,16,256]{3,2,1,0:T(8,128)(2,1)} %bitcast.79), calls=%async_computation.10 | async-start | bytes 1048576 | tf_op jit(solution)/shard_map/all_to_all | solution.py:126
  304.1 1.9 fusion.15
  306.0 16.2 %all-to-all-done.10 = bf16[32,2,16,256]{3,2,1,0:T(8,128)(2,1)S(1)} async-done(((bf16[32,2,16,256]{3,2,1,0:T(8,128)(2,1)}), bf16[32,2,16,256]{3,2,1,0:T(8,128)(2,1)S(1)}, u32[]{:S(2)}, u32[]{:S(2)}) %all-to-all-start.10) | async-done | bytes 524320 | tf_op jit(solution)/shard_map/all_to_all | solution.py:126
  322.2 1.5 fusion.20
  (49 shorter events, 0.7 us)
Async XLA Ops:
  0.0 2.2 copy-start
  0.0 2.5 copy-start.5
  2.6 1.2 copy-start.15
  3.8 0.9 copy-start.7
  3.8 14.0 %copy-start.16 = (bf16[2048,256]{1,0:T(8,128)(2,1)S(1)}, bf16[2048,256]{1,0:T(8,128)(2,1)}, u32[]{:S(2)}) copy-start(bf16[2048,256]{1,0:T(8,128)(2,1)} %param.13) | copy-start | bytes 3145732
  5.6 21.2 %all-to-all-start = ((f32[32,8,128]{2,1,0:T(8,128)}), f32[32,8,128]{2,1,0:T(8,128)S(1)}, u32[]{:S(2)}, u32[]{:S(2)}) async-start(f32[32,8,128]{2,1,0:T(8,128)} %bitcast.3), calls=%async_computation | async-start | bytes 262144 | tf_op jit(solution)/shard_map/all_to_all | solution.py:36
  22.1 13.4 %copy-start.3 = (pred[512,512]{1,0:T(8,128)(4,1)S(1)}, pred[512,512]{1,0:T(8,128)(4,1)}, u32[]{:S(2)}) copy-start(pred[512,512]{1,0:T(8,128)(4,1)} %iota_compare_fusion.9) | copy-start | bytes 786436
  28.8 16.5 %all-to-all-start.1 = ((f32[32,8,128]{2,1,0:T(8,128)}), f32[32,8,128]{2,1,0:T(8,128)S(1)}, u32[]{:S(2)}, u32[]{:S(2)}) async-start(f32[32,8,128]{2,1,0:T(8,128)} %select_reduce_fusion), calls=%async_computation.1 | async-start | bytes 262144 | tf_op jit(solution)/shard_map/all_to_all | solution.py:39
  35.5 14.2 %copy-start.4 = (bf16[512,256]{0,1:T(8,128)(2,1)S(1)}, bf16[512,256]{0,1:T(8,128)(2,1)}, u32[]{:S(2)}) copy-start(bf16[512,256]{0,1:T(8,128)(2,1)} %convolution_convert_fusion.2) | copy-start | bytes 786436
  45.3 20.3 %all-to-all-start.3 = ((bf16[256,8,256]{2,0,1:T(8,128)(2,1)}), bf16[256,8,256]{2,0,1:T(8,128)(2,1)}, u32[]{:S(2)}, u32[]{:S(2)}) async-start(bf16[256,8,256]{2,0,1:T(8,128)(2,1)} %copy.65), calls=%async_computation.3 | async-start | bytes 2097152 | tf_op jit(solution)/shard_map/all_to_all | solution.py:23
  49.7 1.0 copy-start.6
  67.1 3.8 %copy-start.14 = (s32[512,1]{0,1:T(1,128)S(1)}, s32[512,1]{0,1:T(1,128)}, u32[]{:S(2)}) copy-start(s32[512,1]{0,1:T(1,128)} %param.23) | copy-start | bytes 6148
  67.1 30.8 %all-to-all-start.2 = ((bf16[8,512,256]{2,1,0:T(8,128)(2,1)}), bf16[8,512,256]{2,1,0:T(8,128)(2,1)S(1)}, u32[]{:S(2)}, u32[]{:S(2)}) async-start(bf16[8,512,256]{2,1,0:T(8,128)(2,1)} %stack.8), calls=%async_computation.2 | async-start | bytes 4194304 | tf_op jit(solution)/shard_map/all_to_all | solution.py:28
  102.0 22.2 %all-to-all-start.5 = ((bf16[32,2,16,256]{3,2,1,0:T(8,128)(2,1)}), bf16[32,2,16,256]{3,2,1,0:T(8,128)(2,1)S(1)}, u32[]{:S(2)}, u32[]{:S(2)}) async-start(bf16[32,2,16,256]{3,2,1,0:T(8,128)(2,1)} %bitcast.15), calls=%async_computation.5 | async-start | bytes 1048576 | tf_op jit(solution)/shard_map/all_to_all | solution.py:103
  125.7 30.7 %all-to-all-start.4 = ((bf16[8,512,256]{1,2,0:T(8,128)(2,1)}), bf16[8,512,256]{1,2,0:T(8,128)(2,1)S(1)}, u32[]{:S(2)}, u32[]{:S(2)}) async-start(bf16[8,512,256]{1,2,0:T(8,128)(2,1)} %stack.9), calls=%async_computation.4 | async-start | bytes 4194304 | tf_op jit(solution)/shard_map/all_to_all | solution.py:28
  158.7 4.7 %copy-start.8 = (bf16[2,128,2048]{2,1,0:T(8,128)(2,1)S(1)}, bf16[2,128,2048]{2,1,0:T(8,128)(2,1)}, u32[]{:S(2)}) copy-start(bf16[2,128,2048]{2,1,0:T(8,128)(2,1)} %param.22) | copy-start | bytes 3145732
  158.7 54.3 %all-to-all-start.6 = ((bf16[8,1024,256]{2,1,0:T(8,128)(2,1)}), bf16[8,1024,256]{2,1,0:T(8,128)(2,1)}, u32[]{:S(2)}, u32[]{:S(2)}) async-start(bf16[8,1024,256]{2,1,0:T(8,128)(2,1)} %stack.10), calls=%async_computation.6 | async-start | bytes 8388608 | tf_op jit(solution)/shard_map/all_to_all | solution.py:28
  165.4 1.0 copy-start.13
  165.4 1.8 copy-start.18
  213.0 25.9 %all-to-all-start.9 = ((bf16[2,128,2048]{1,0,2:T(2,128)(2,1)}), bf16[2,128,2048]{1,0,2:T(2,128)(2,1)S(1)}, u32[]{:S(2)}, u32[]{:S(2)}) async-start(bf16[2,128,2048]{1,0,2:T(2,128)(2,1)} %copy.72), calls=%async_computation.9 | async-start | bytes 2097152 | tf_op jit(solution)/shard_map/all_to_all | solution.py:71
  226.4 7.5 %copy-start.10 = (bf16[2,2048,128]{2,1,0:T(8,128)(2,1)S(1)}, bf16[2,2048,128]{2,1,0:T(8,128)(2,1)}, u32[]{:S(2)}) copy-start(bf16[2,2048,128]{2,1,0:T(8,128)(2,1)} %param.20) | copy-start | bytes 3145732
  233.9 3.6 %copy-start.2 = (bf16[2,512,2048]{2,1,0:T(8,128)(2,1)S(1)}, bf16[2,512,2048]{2,1,0:T(8,128)(2,1)}, u32[]{:S(2)}) copy-start(bf16[2,512,2048]{2,1,0:T(8,128)(2,1)} %reshape_reshape.3) | copy-start | bytes 12582916
  233.9 3.7 %copy-start.17 = (bf16[2,2048,128]{2,1,0:T(8,128)(2,1)S(1)}, bf16[2,2048,128]{2,1,0:T(8,128)(2,1)}, u32[]{:S(2)}) copy-start(bf16[2,2048,128]{2,1,0:T(8,128)(2,1)} %param.21) | copy-start | bytes 3145732
  241.0 4.9 %copy-start.12 = (bf16[128,2048]{1,0:T(8,128)(2,1)S(1)}, bf16[128,2048]{1,0:T(8,128)(2,1)}, u32[]{:S(2)}) copy-start(bf16[128,2048]{1,0:T(8,128)(2,1)} %param.19) | copy-start | bytes 1572868
  241.0 43.4 %all-to-all-start.7 = ((bf16[8,1536,128]{2,1,0:T(8,128)(2,1)}), bf16[8,1536,128]{2,1,0:T(8,128)(2,1)}, u32[]{:S(2)}, u32[]{:S(2)}) async-start(bf16[8,1536,128]{2,1,0:T(8,128)(2,1)} %stack.11), calls=%async_computation.7 | async-start | bytes 6291456 | tf_op jit(solution)/shard_map/all_to_all | solution.py:28
  284.4 14.8 %all-to-all-start.8 = ((bf16[128,8,256]{2,0,1:T(8,128)(2,1)}), bf16[128,8,256]{2,0,1:T(8,128)(2,1)}, u32[]{:S(2)}, u32[]{:S(2)}) async-start(bf16[128,8,256]{2,0,1:T(8,128)(2,1)} %copy.70), calls=%async_computation.8 | async-start | bytes 1048576 | tf_op jit(solution)/shard_map/all_to_all | solution.py:23
  293.7 2.3 copy-start.9
  296.0 8.1 %copy-start.11 = (f32[512,256]{1,0:T(8,128)S(1)}, f32[512,256]{1,0:T(8,128)}, u32[]{:S(2)}) copy-start(f32[512,256]{1,0:T(8,128)} %get-tuple-element.8) | copy-start | bytes 1572868
  299.2 23.1 %all-to-all-start.10 = ((bf16[32,2,16,256]{3,2,1,0:T(8,128)(2,1)}), bf16[32,2,16,256]{3,2,1,0:T(8,128)(2,1)S(1)}, u32[]{:S(2)}, u32[]{:S(2)}) async-start(bf16[32,2,16,256]{3,2,1,0:T(8,128)(2,1)} %bitcast.79), calls=%async_computation.10 | async-start | bytes 1048576 | tf_op jit(solution)/shard_map/all_to_all | solution.py:126
  304.1 19.7 %copy-start.1 = (bf16[2048,256]{1,0:T(8,128)(2,1)S(1)}, bf16[2048,256]{1,0:T(8,128)(2,1)}, u32[]{:S(2)}) copy-start(bf16[2048,256]{1,0:T(8,128)(2,1)} %param.14) | copy-start | bytes 3145732
